TPU v7x, 512 devices: a whole 4x8x8 slice. The times are simulated.
512 devices in a mesh: mod: 2 (over z_hi), loop: 16 (over x, z_lo), line: 16 (over y, core).
Axes of the slice: x: 4, y: 8, z: 8 (z_hi: 2, z_lo: 4; z = z_hi * 4 + z_lo), core: 2. Of those that a mesh axis runs over, the one named last changes fastest.
Arguments:
- act: bfloat16 [2, 196608, 512], P('mod', ('loop', 'line'))
- dy: bfloat16 [2, 196608, 1280], P('mod', ('loop', 'line')), may hold values from -6 to 6
- w_out: bfloat16 [2, 512, 1280], P('mod'), may hold values from -0.15625 to 0.15625
- counts: int32 [2, 16, 16], P('mod', 'loop', 'line'), may hold values from 192 to 768, as said below
Outputs:
- grad_clipped: float32 [2, 512, 1280], P('mod', 'loop')
- hidden_grad: bfloat16 [2, 196608, 512], P('mod', ('loop', 'line'))
Inputs may be any that keep to these rules, and one draw needn't show every extreme that they name: `counts`: in each tower some device has all 768 slots live.
All inputs are finite; a program needn't handle non-finite values.
Results may differ from a plain program's by a relative error of at most 0.001.
Values sent between devices are 32-bit elements; how exact they have to be, the bound alone decides.
A program may use at most 64 MiB of HBM per device.

v0:
```python
import jax
import jax.numpy as jnp
from jax import lax
from jax.sharding import PartitionSpec as P


def on_device(act, dy, w_out, counts):
    tokens = act[0]
    upstream = dy[0]
    weight = w_out[0]
    rows = tokens.shape[0]
    hidden = tokens.shape[1]
    block = weight.shape[1]
    live = lax.broadcasted_iota(jnp.int32, (rows, 1), 0) < counts[0, 0]
    masked = jnp.where(live, tokens, jnp.zeros_like(tokens))
    entries = lax.axis_size("mod") * hidden * block
    share = lax.psum_scatter(
        lax.dot_general(
            masked, upstream, (((0,), (0,)), ((), ())), preferred_element_type=jnp.float32
        ),
        "loop",
        scatter_dimension=0,
        tiled=True,
    )
    share = lax.psum(share, "line")
    total = lax.psum(jnp.sum(share * share), ("mod", "loop"))
    factor = 1.0 / jnp.sqrt(total / entries + 1e-06)
    clipped = share * factor
    back = lax.dot_general(
        upstream, weight, (((1,), (1,)), ((), ())), preferred_element_type=jnp.float32
    )
    hidden_grad = jnp.where(live, back, jnp.zeros_like(back)).astype(jnp.bfloat16)
    return (clipped[None], hidden_grad[None])


def solution(mesh):
    in_specs = (
        P("mod", ("loop", "line"), None),
        P("mod", ("loop", "line"), None),
        P("mod", None, None),
        P("mod", "loop", "line"),
    )
    out_specs = (P("mod", "loop", None), P("mod", ("loop", "line"), None))
    return jax.shard_map(
        on_device, mesh=mesh, in_specs=in_specs, out_specs=out_specs, check_vma=False
    )
```

profile of v0, /device:TPU:8, one launch (start us, length us, event | category | flops | bytes accessed | tf_op | source)
XLA Modules:
  0.0 310.6 jit_solution(13326542029925265666)
XLA Ops:
  7.2 0.0 copy-start
  7.2 0.0 reduce-scatter.2.cloned.1.call-start
  8.0 0.7 copy-done
  8.7 3.9 %fusion.2 = f32[512,1280]{1,0:T(8,128)} fusion(bf16[1,768,1280]{2,1,0:T(8,128)(2,1)S(1)} %copy-done, bf16[1,768,512]{2,1,0:T(8,128)(2,1)} %param.4, pred[768]{0:T(1024)(128)(4,1)S(1)} %iota_compare_fusion), kind=kOutput, calls=%fused_computation.2 | convolution fusion | flops 1007026176 | bytes 5374720 | tf_op jit(solution)/shard_map/dot_general | solution.py:18
  12.7 0.0 copy-start.2
  12.7 0.0 reduce-scatter.2.cloned.1.call-update
  12.7 0.0 all-reduce.2.cloned.1.call-start
  12.8 101.7 %reduce-scatter.2.cloned.1.call-done = f32[32,1280]{1,0:T(8,128)} async-done(((f32[512,1280]{1,0:T(8,128)}), f32[32,1280]{1,0:T(8,128)}) %reduce-scatter.2.cloned.1.call-update) | async-done | bytes 163856 | tf_op jit(solution)/shard_map/reduce_scatter | solution.py:17
  114.5 0.0 all-reduce.2.cloned.1.call-update
  114.5 108.3 %all-reduce.2.cloned.1.call-done = f32[32,1280]{1,0:T(8,128)} async-done(((f32[32,1280]{1,0:T(8,128)}), f32[32,1280]{1,0:T(8,128)}) %all-reduce.2.cloned.1.call-update) | async-done | bytes 163856 | tf_op jit(solution)/shard_map/psum | solution.py:25
  222.8 1.6 multiply_reduce_fusion
  224.4 0.0 copy-done.2
  224.4 0.0 copy-start.1
  224.4 2.1 fusion.7
  226.5 75.9 %psum.15 = f32[]{:T(128)} all-reduce(f32[]{:T(128)} %multiply_reduce_fusion), channel_id=1, replica_groups=mesh['mod'=2,'loop'=16,'line'=16] {'mod','loop'}, use_global_device_ids=true, to_apply=%region_3.4 | all-reduce | flops 1 | bytes 8 | tf_op jit(solution)/shard_map/psum | solution.py:26
  303.1 0.0 copy-done.1
  303.1 0.7 multiply_bitcast_fusion
  (1 shorter events, 0.0 us)
Async XLA Ops:
  7.2 1.6 copy-start
  7.2 107.3 %reduce-scatter.2.cloned.1.call-start = ((), (), s32[]{:S(2)}) async-start(), calls=%async_computation.1 | async-start | bytes 2785280 | tf_op jit(solution)/shard_map/reduce_scatter | solution.py:17
  12.7 211.7 %copy-start.2 = (bf16[1,512,1280]{2,1,0:T(8,128)(2,1)S(1)}, bf16[1,512,1280]{2,1,0:T(8,128)(2,1)}, u32[]{:S(2)}) copy-start(bf16[1,512,1280]{2,1,0:T(8,128)(2,1)} %param.6) | copy-start | bytes 3932164
  12.7 210.1 %all-reduce.2.cloned.1.call-start = ((), (), s32[]{:S(2)}) async-start(), calls=%async_computation.2 | async-start | bytes 327680 | tf_op jit(solution)/shard_map/psum | solution.py:25
  224.4 78.7 %copy-start.1 = (f32[32,1280]{1,0:T(8,128)S(1)}, f32[32,1280]{1,0:T(8,128)}, u32[]{:S(2)}) copy-start(f32[32,1280]{1,0:T(8,128)} %all-reduce.2.cloned.1.call-done) | copy-start | bytes 491524
Sparse Core Ops, SparseCore 0:
  12.8 101.6 reduce-scatter.1
  116.8 105.9 all-reduce.1
where the time goes:
time: 311 us
  waiting for transfers between devices  210 us (68%)
  blocking collectives  75.9 us (24%)
  between operations  15.5 us (5%)
  matrix products  6.04 us (2%)
    psum x1, waiting for transfers between devices, on_device(): share = lax.psum(share, 'line')  108 us
    reduce_scatter x1, waiting for transfers between devices, on_device(): lax.psum_scatter(lax.dot_general(masked, upstream, (((0,), (0,)), ((), ()...  102 us
    psum x1, blocking collectives, on_device(): total = lax.psum(jnp.sum(share * share), ('mod', 'loop'))  75.9 us
  transfers between devices with their start and end apart: 2, of which 2 were waited for; matrix products, arithmetic and copies ran while one was open for 0% of the time, Pallas kernels for 0%

commit v1 on v0

--- a/solution.py
+++ b/solution.py
@@ -2,6 +2,15 @@
 import jax.numpy as jnp
 from jax import lax
 from jax.sharding import PartitionSpec as P
+
+
+def add_in_pairs(x, axis):
+    count = lax.axis_size(axis)
+    acc, hop = (x, 1)
+    while hop < count:
+        acc = acc + lax.ppermute(acc, axis, [(i, i ^ hop) for i in range(count)])
+        hop = 2 * hop
+    return acc
 
 
 def on_device(act, dy, w_out, counts):
@@ -22,7 +31,7 @@
         scatter_dimension=0,
         tiled=True,
     )
-    share = lax.psum(share, "line")
+    share = add_in_pairs(share, "line")
     total = lax.psum(jnp.sum(share * share), ("mod", "loop"))
     factor = 1.0 / jnp.sqrt(total / entries + 1e-06)
     clipped = share * factor

time: 311 us -> 236 us (0.76)
  the two profiles are of different devices: /device:TPU:8 before, /device:TPU:56 now
where the time goes in v1:
time: 236 us
  waiting for transfers between devices  123 us (52%)
  blocking collectives  74.1 us (31%)
  between operations  15.6 us (7%)
  starting transfers between devices  14.4 us (6%)
  matrix products  6.05 us (3%)
    reduce_scatter x1, waiting for transfers between devices, on_device(): lax.psum_scatter(lax.dot_general(masked, upstream, (((0,), (0,)), ((), ()...  101 us
    psum x1, blocking collectives, on_device(): total = lax.psum(jnp.sum(share * share), ('mod', 'loop'))  74.1 us
    ppermute x4, waiting for transfers between devices, add_in_pairs(): acc = acc + lax.ppermute(acc, axis, [(i, i ^ hop) for i in range(count)])  21.6 us
    ppermute x4, starting transfers between devices, add_in_pairs(): acc = acc + lax.ppermute(acc, axis, [(i, i ^ hop) for i in range(count)])  14.4 us
  transfers between devices with their start and end apart: 5, of which 5 were waited for; matrix products, arithmetic and copies ran while one was open for 1% of the time, Pallas kernels for 0%

profile of v1, /device:TPU:56, one launch (start us, length us, event | category | flops | bytes accessed | tf_op | source)
XLA Modules:
  0.0 235.7 jit_solution(17020692300539463405)
XLA Ops:
  7.2 0.0 copy-start
  7.2 0.0 reduce-scatter.2.cloned.1.call-start
  8.0 0.7 copy-done
  8.7 4.0 %fusion.2 = f32[512,1280]{1,0:T(8,128)} fusion(bf16[1,768,1280]{2,1,0:T(8,128)(2,1)S(1)} %copy-done, bf16[1,768,512]{2,1,0:T(8,128)(2,1)} %param.4, pred[768]{0:T(1024)(128)(4,1)S(1)} %iota_compare_fusion), kind=kOutput, calls=%fused_computation.2 | convolution fusion | flops 1007026176 | bytes 5374720 | tf_op jit(solution)/shard_map/dot_general | solution.py:27
  12.7 0.0 copy-start.1
  12.7 0.0 reduce-scatter.2.cloned.1.call-update
  12.7 100.9 %reduce-scatter.2.cloned.1.call-done = f32[32,1280]{1,0:T(8,128)} async-done(((f32[512,1280]{1,0:T(8,128)}), f32[32,1280]{1,0:T(8,128)}) %reduce-scatter.2.cloned.1.call-update) | async-done | bytes 163856 | tf_op jit(solution)/shard_map/reduce_scatter | solution.py:26
  113.7 1.9 collective-permute-start
  115.6 1.6 collective-permute-done
  117.1 0.9 add.19
  118.1 3.2 %collective-permute-start.1 = (f32[32,1280]{1,0:T(8,128)S(1)}, f32[32,1280]{1,0:T(8,128)S(1)}, u32[]{:S(2)}, u32[]{:S(2)}) collective-permute-start(f32[32,1280]{1,0:T(8,128)S(1)} %add.19), channel_id=1, source_target_pairs={{0,2},{1,3},{2,0},{3,1},{4,6},{5,7},{6,4},{7,5},{8,10},{9,11},{10,... | collective-permute-start | bytes 491528 | tf_op jit(solution)/shard_map/ppermute | solution.py:11
  121.3 4.9 %collective-permute-done.1 = f32[32,1280]{1,0:T(8,128)S(1)} collective-permute-done((f32[32,1280]{1,0:T(8,128)S(1)}, f32[32,1280]{1,0:T(8,128)S(1)}, u32[]{:S(2)}, u32[]{:S(2)}) %collective-permute-start.1) | collective-permute-done | bytes 163872 | tf_op jit(solution)/shard_map/ppermute | solution.py:11
  126.3 4.5 %collective-permute-start.2 = (f32[32,1280]{1,0:T(8,128)S(1)}, f32[32,1280]{1,0:T(8,128)S(1)}, u32[]{:S(2)}, u32[]{:S(2)}) collective-permute-start(f32[32,1280]{1,0:T(8,128)S(1)} %add.20), channel_id=1, source_target_pairs={{0,4},{1,5},{2,6},{3,7},{4,0},{5,1},{6,2},{7,3},{8,12},{9,13},{10,... | collective-permute-start | bytes 491528 | tf_op jit(solution)/shard_map/ppermute | solution.py:11
  130.8 7.4 %collective-permute-done.2 = f32[32,1280]{1,0:T(8,128)S(1)} collective-permute-done((f32[32,1280]{1,0:T(8,128)S(1)}, f32[32,1280]{1,0:T(8,128)S(1)}, u32[]{:S(2)}, u32[]{:S(2)}) %collective-permute-start.2) | collective-permute-done | bytes 163872 | tf_op jit(solution)/shard_map/ppermute | solution.py:11
  138.2 4.7 %collective-permute-start.3 = (f32[32,1280]{1,0:T(8,128)S(1)}, f32[32,1280]{1,0:T(8,128)S(1)}, u32[]{:S(2)}, u32[]{:S(2)}) collective-permute-start(f32[32,1280]{1,0:T(8,128)S(1)} %add.21), channel_id=1, source_target_pairs={{0,8},{1,9},{2,10},{3,11},{4,12},{5,13},{6,14},{7,15},{8,0},{9,1},... | collective-permute-start | bytes 491528 | tf_op jit(solution)/shard_map/ppermute | solution.py:11
  142.9 0.0 copy-done.1
  143.0 2.1 fusion.7
  145.0 7.7 %collective-permute-done.3 = f32[32,1280]{1,0:T(8,128)S(1)} collective-permute-done((f32[32,1280]{1,0:T(8,128)S(1)}, f32[32,1280]{1,0:T(8,128)S(1)}, u32[]{:S(2)}, u32[]{:S(2)}) %collective-permute-start.3) | collective-permute-done | bytes 163872 | tf_op jit(solution)/shard_map/ppermute | solution.py:11
  152.7 0.6 multiply_reduce_fusion
  153.4 74.1 %psum.7 = f32[]{:T(128)} all-reduce(f32[]{:T(128)} %get-tuple-element.2), channel_id=1, replica_groups=mesh['mod'=2,'loop'=16,'line'=16] {'mod','loop'}, use_global_device_ids=true, to_apply=%region_2.3 | all-reduce | flops 1 | bytes 8 | tf_op jit(solution)/shard_map/psum | solution.py:35
  228.2 0.7 multiply_bitcast_fusion
  (3 shorter events, 0.0 us)
Async XLA Ops:
  7.2 1.6 copy-start
  7.2 106.5 %reduce-scatter.2.cloned.1.call-start = ((), (), s32[]{:S(2)}) async-start(), calls=%async_computation.1 | async-start | bytes 2785280 | tf_op jit(solution)/shard_map/reduce_scatter | solution.py:26
  12.7 130.3 %copy-start.1 = (bf16[1,512,1280]{2,1,0:T(8,128)(2,1)S(1)}, bf16[1,512,1280]{2,1,0:T(8,128)(2,1)}, u32[]{:S(2)}) copy-start(bf16[1,512,1280]{2,1,0:T(8,128)(2,1)} %param.6) | copy-start | bytes 3932164
  113.7 3.5 %collective-permute-start = (f32[32,1280]{1,0:T(8,128)}, f32[32,1280]{1,0:T(8,128)S(1)}, u32[]{:S(2)}, u32[]{:S(2)}) collective-permute-start(f32[32,1280]{1,0:T(8,128)} %reduce-scatter.2.cloned.1.call-done), channel_id=1, source_target_pairs={{0,1},{1,0},{2,3},{3,2},{4,5},{5,4},{6,7},{7,6},{8,9},{9,8},{10,11... | collective-permute-start | bytes 491528 | tf_op jit(solution)/shard_map/ppermute | solution.py:11
  118.1 8.1 %collective-permute-start.1 = (f32[32,1280]{1,0:T(8,128)S(1)}, f32[32,1280]{1,0:T(8,128)S(1)}, u32[]{:S(2)}, u32[]{:S(2)}) collective-permute-start(f32[32,1280]{1,0:T(8,128)S(1)} %add.19), channel_id=1, source_target_pairs={{0,2},{1,3},{2,0},{3,1},{4,6},{5,7},{6,4},{7,5},{8,10},{9,11},{10,... | collective-permute-start | bytes 491528 | tf_op jit(solution)/shard_map/ppermute | solution.py:11
  126.3 12.0 %collective-permute-start.2 = (f32[32,1280]{1,0:T(8,128)S(1)}, f32[32,1280]{1,0:T(8,128)S(1)}, u32[]{:S(2)}, u32[]{:S(2)}) collective-permute-start(f32[32,1280]{1,0:T(8,128)S(1)} %add.20), channel_id=1, source_target_pairs={{0,4},{1,5},{2,6},{3,7},{4,0},{5,1},{6,2},{7,3},{8,12},{9,13},{10,... | collective-permute-start | bytes 491528 | tf_op jit(solution)/shard_map/ppermute | solution.py:11
  138.2 14.5 %collective-permute-start.3 = (f32[32,1280]{1,0:T(8,128)S(1)}, f32[32,1280]{1,0:T(8,128)S(1)}, u32[]{:S(2)}, u32[]{:S(2)}) collective-permute-start(f32[32,1280]{1,0:T(8,128)S(1)} %add.21), channel_id=1, source_target_pairs={{0,8},{1,9},{2,10},{3,11},{4,12},{5,13},{6,14},{7,15},{8,0},{9,1},... | collective-permute-start | bytes 491528 | tf_op jit(solution)/shard_map/ppermute | solution.py:11
Sparse Core Ops, SparseCore 0:
  12.8 100.7 reduce-scatter.1
